TPU v7x, 128 devices: a whole 4x4x4 slice. The times are simulated.
128 devices in a mesh: cluster: 16 (over y, x_lo, core), blk: 8 (over x_hi, z).
Axes of the slice: x: 4 (x_hi: 2, x_lo: 2; x = x_hi * 2 + x_lo), y: 4, z: 4, core: 2. Of those that a mesh axis runs over, the one named last changes fastest.
Arguments:
- embeds: bfloat16 [4096, 32, 128], P(('cluster', 'blk')), may hold values from -7 to 7
- labels: int32 [4096, 1], P(('cluster', 'blk')), may hold values from 0 to 15, as said below
- keep: int32 [4096], P(('cluster', 'blk')), may hold values 0 or 1
Outputs:
- dup_score: float32 [4096], P(('cluster', 'blk'))
Inputs may be any that keep to these rules, and one draw needn't show every extreme that they name: `labels`: at most 4 prompts of one device carry the same label, and on every device some label is carried by exactly 4 of its prompts.
All inputs are finite; a program needn't handle non-finite values. No bound on the sum of `keep` on one device may be relied on, other than what follows from the above.
Results may differ from a plain program's by a relative error of at most 0.0003.
Values may be sent and summed in bfloat16 or wider, within the bound.
A program may use at most 64 MiB of HBM per device.

v0:
```python
import jax
import jax.numpy as jnp
from jax import lax
from jax.sharding import PartitionSpec as P

SLOTS = 64


group_size = 8


def pair_scores(residents, visitors):
    length = residents.shape[1]
    width = residents.shape[2]
    visiting = visitors.shape[0]
    flat_visitors = visitors.reshape(visiting * length, width)
    grouped = residents.reshape(residents.shape[0] // group_size, group_size * length, width)

    def one_group(queries):
        score_tile = lax.dot_general(
            queries, flat_visitors, (((1,), (1,)), ((), ())), preferred_element_type=jnp.float32
        )
        score_tile = score_tile.reshape(group_size, length, visiting, length)
        forward = jnp.sum(jnp.max(score_tile, axis=3), axis=1) / length
        return forward

    result = lax.map(one_group, grouped)
    return result.reshape(-1, visiting)


def body(embeds, labels, keep):
    clusters = lax.axis_size("cluster")
    slot_count = SLOTS
    capacity = slot_count // clusters
    label_list = labels[:, 0]
    onehot = (label_list[:, None] == jnp.arange(clusters, dtype=jnp.int32)[None, :]).astype(
        jnp.int32
    )
    slot_rank = jnp.sum((jnp.cumsum(onehot, axis=0) - onehot) * onehot, axis=1)
    slot_index = label_list * capacity + slot_rank
    keep_float = keep.astype(jnp.float32)
    outgoing = (
        jnp.zeros((slot_count, embeds.shape[1], embeds.shape[2]), jnp.bfloat16)
        .at[slot_index]
        .set(embeds)
    )
    outgoing_flags = (
        jnp.zeros((slot_count,), jnp.bfloat16).at[slot_index].set(keep.astype(jnp.bfloat16))
    )
    members, member_flags = (
        lax.all_to_all(outgoing, "cluster", split_axis=0, concat_axis=0, tiled=True),
        lax.all_to_all(outgoing_flags, "cluster", split_axis=0, concat_axis=0, tiled=True),
    )
    flags = member_flags.astype(jnp.float32)
    own_ids = lax.axis_index("blk") * slot_count + jnp.arange(slot_count, dtype=jnp.int32)
    visitors = lax.all_gather(members, "blk", axis=0, tiled=True)
    visitor_flags = lax.all_gather(member_flags, "blk", axis=0, tiled=True)
    other_ids = jnp.arange(visitors.shape[0], dtype=jnp.int32)
    weights = (own_ids[:, None] != other_ids[None, :]).astype(jnp.float32) * visitor_flags.astype(
        jnp.float32
    )[None, :]
    forward = pair_scores(members, visitors)
    sums = jnp.sum(forward * weights, axis=1)
    counts = jnp.sum(weights, axis=1)
    score = jnp.where(flags > 0, sums / jnp.maximum(counts, 1.0), 0.0)
    returned = lax.all_to_all(score, "cluster", split_axis=0, concat_axis=0, tiled=True)
    return returned[slot_index] * keep_float


def solution(mesh):
    return jax.shard_map(
        body,
        mesh=mesh,
        in_specs=(
            P(("cluster", "blk"), None, None),
            P(("cluster", "blk"), None),
            P(("cluster", "blk")),
        ),
        out_specs=P(("cluster", "blk")),
        check_vma=False,
    )
```

profile of v0, /device:TPU:0, one launch (start us, length us, event | category | flops | bytes accessed | tf_op | source)
XLA Modules:
  0.0 190.5 jit_solution(1213588134446596878)
XLA Ops:
  6.5 0.0 all-gather.2.cloned.1.call-start
  6.5 0.7 fusion.6
  7.3 0.1 reduce_window_sum.11
  7.3 0.8 select_reduce_fusion.1
  8.2 0.7 fusion.7
  8.8 0.1 broadcast_in_dim.11
  8.9 2.8 %scatter_fusion = bf16[64,32,128]{2,1,0:T(8,128)(2,1)S(1)} fusion(bf16[64,32,128]{2,1,0:T(8,128)(2,1)S(1)} %broadcast_in_dim.11, s32[32]{0:T(128)S(1)} %fusion.7, bf16[32,32,128]{2,1,0:T(8,128)(2,1)} %param.5), kind=kCustom, calls=%fused_computation.2 | custom fusion | bytes 786560 | tf_op jit(solution)/shard_map/scatter | solution.py:45
  11.7 16.4 %all_to_all.27 = bf16[64,32,128]{2,1,0:T(8,128)(2,1)} all-to-all(bf16[64,32,128]{2,1,0:T(8,128)(2,1)S(1)} %scatter_fusion), channel_id=1, replica_groups=mesh['cluster'=16,'blk'=8] {'cluster'}, dimensions={0} | all-to-all | bytes 1048576 | tf_op jit(solution)/shard_map/all_to_all | solution.py:51
  28.1 0.0 all-gather.2.cloned.1.call-update
  28.1 0.7 convert_element_type.18
  28.8 0.8 scatter_custom_fusion
  29.6 0.7 all_to_all.23
  30.3 3.4 %all-to-all-start = ((bf16[16,4,1]{1,2,0:T(2,128)(2,1)}), bf16[16,4,1]{1,2,0:T(2,128)(2,1)S(1)}, u32[]{:S(2)}, u32[]{:S(2)}) async-start(bf16[16,4,1]{1,2,0:T(2,128)(2,1)} %all_to_all.23), calls=%async_computation | async-start | bytes 16384 | tf_op jit(solution)/shard_map/all_to_all | solution.py:52
  33.7 1.3 dynamic-slice
  35.6 4.0 %all-to-all-done = bf16[16,4,1]{1,2,0:T(2,128)(2,1)S(1)} async-done(((bf16[16,4,1]{1,2,0:T(2,128)(2,1)}), bf16[16,4,1]{1,2,0:T(2,128)(2,1)S(1)}, u32[]{:S(2)}, u32[]{:S(2)}) %all-to-all-start) | async-done | bytes 160 | tf_op jit(solution)/shard_map/all_to_all | solution.py:52
  39.7 0.1 reshape.94
  39.8 0.2 dynamic-update-slice
  40.0 25.2 %all-reduce = bf16[512]{0:T(512)(128)(2,1)S(1)} all-reduce(bf16[512]{0:T(512)(128)(2,1)S(1)} %dynamic-update-slice), channel_id=1, replica_groups=mesh['cluster'=16,'blk'=8] {'blk'}, use_global_device_ids=true, to_apply=%add | all-reduce | flops 512 | bytes 2048
  65.2 0.2 select_reduce_fusion
  65.4 0.1 max.18
  65.5 34.2 %all-gather.2.cloned.1.call-done = bf16[512,32,128]{2,1,0:T(8,128)(2,1)} async-done(((bf16[64,32,128]{2,1,0:T(8,128)(2,1)}), bf16[512,32,128]{2,1,0:T(8,128)(2,1)}) %all-gather.2.cloned.1.call-update) | async-done | bytes 4194320 | tf_op jit(solution)/shard_map/all_gather | solution.py:56
  99.7 0.0 copy-start
  99.7 70.3 %while.11 = (s32[]{:T(128)}, f32[8,8,512]{2,1,0:T(8,128)S(1)}, bf16[8,256,128]{2,1,0:T(8,128)(2,1)}, bf16[16384,128]{1,0:T(8,128)(2,1)}) while((s32[]{:T(128)}, f32[8,8,512]{2,1,0:T(8,128)S(1)}, bf16[8,256,128]{2,1,0:T(8,128)(2,1)}, bf16[16384,128]{1,0:T(8,128)(2,1)}) %tuple.27), condition=%wide.region_7.8_spmd.clone, body=%wide.region_4.7_spmd.sunk.clone | while | flops 1077936128 | bytes 5488705 | solution.py:27
  99.7 0.9 constant_dynamic-slice_fusion.3
  100.5 7.8 %fusion.19 = f32[8,32,512]{2,1,0:T(8,128)S(1)} fusion(bf16[8,32,128,1]{2,1,3,0:T(8,128)(2,1)S(1)} %bitcast.42, bf16[512,32,128]{2,1,0:T(8,128)(2,1)} %bitcast.46), kind=kOutput, calls=%fused_computation.6.clone.1.clone | convolution fusion | flops 1077805056 | bytes 4784128 | tf_op jit(solution)/shard_map/while/body/eval_jaxpr/dot_general | solution.py:20
  108.4 0.1 reduce_sum.50
  108.5 0.8 constant_dynamic-slice_fusion.3
  109.3 7.8 %fusion.19 = f32[8,32,512]{2,1,0:T(8,128)S(1)} fusion(bf16[8,32,128,1]{2,1,3,0:T(8,128)(2,1)S(1)} %bitcast.42, bf16[512,32,128]{2,1,0:T(8,128)(2,1)} %bitcast.46), kind=kOutput, calls=%fused_computation.6.clone.1.clone | convolution fusion | flops 1077805056 | bytes 4784128 | tf_op jit(solution)/shard_map/while/body/eval_jaxpr/dot_general | solution.py:20
  117.2 0.1 reduce_sum.50
  117.3 0.8 constant_dynamic-slice_fusion.3
  118.1 7.8 %fusion.19 = f32[8,32,512]{2,1,0:T(8,128)S(1)} fusion(bf16[8,32,128,1]{2,1,3,0:T(8,128)(2,1)S(1)} %bitcast.42, bf16[512,32,128]{2,1,0:T(8,128)(2,1)} %bitcast.46), kind=kOutput, calls=%fused_computation.6.clone.1.clone | convolution fusion | flops 1077805056 | bytes 4784128 | tf_op jit(solution)/shard_map/while/body/eval_jaxpr/dot_general | solution.py:20
  125.9 0.1 reduce_sum.50
  126.0 0.8 constant_dynamic-slice_fusion.3
  126.9 7.8 %fusion.19 = f32[8,32,512]{2,1,0:T(8,128)S(1)} fusion(bf16[8,32,128,1]{2,1,3,0:T(8,128)(2,1)S(1)} %bitcast.42, bf16[512,32,128]{2,1,0:T(8,128)(2,1)} %bitcast.46), kind=kOutput, calls=%fused_computation.6.clone.1.clone | convolution fusion | flops 1077805056 | bytes 4784128 | tf_op jit(solution)/shard_map/while/body/eval_jaxpr/dot_general | solution.py:20
  134.7 0.1 reduce_sum.50
  134.8 0.8 constant_dynamic-slice_fusion.3
  135.7 7.8 %fusion.19 = f32[8,32,512]{2,1,0:T(8,128)S(1)} fusion(bf16[8,32,128,1]{2,1,3,0:T(8,128)(2,1)S(1)} %bitcast.42, bf16[512,32,128]{2,1,0:T(8,128)(2,1)} %bitcast.46), kind=kOutput, calls=%fused_computation.6.clone.1.clone | convolution fusion | flops 1077805056 | bytes 4784128 | tf_op jit(solution)/shard_map/while/body/eval_jaxpr/dot_general | solution.py:20
  143.5 0.1 reduce_sum.50
  143.6 0.8 constant_dynamic-slice_fusion.3
  144.5 7.8 %fusion.19 = f32[8,32,512]{2,1,0:T(8,128)S(1)} fusion(bf16[8,32,128,1]{2,1,3,0:T(8,128)(2,1)S(1)} %bitcast.42, bf16[512,32,128]{2,1,0:T(8,128)(2,1)} %bitcast.46), kind=kOutput, calls=%fused_computation.6.clone.1.clone | convolution fusion | flops 1077805056 | bytes 4784128 | tf_op jit(solution)/shard_map/while/body/eval_jaxpr/dot_general | solution.py:20
  152.3 0.1 reduce_sum.50
  152.4 0.8 constant_dynamic-slice_fusion.3
  153.2 7.8 %fusion.19 = f32[8,32,512]{2,1,0:T(8,128)S(1)} fusion(bf16[8,32,128,1]{2,1,3,0:T(8,128)(2,1)S(1)} %bitcast.42, bf16[512,32,128]{2,1,0:T(8,128)(2,1)} %bitcast.46), kind=kOutput, calls=%fused_computation.6.clone.1.clone | convolution fusion | flops 1077805056 | bytes 4784128 | tf_op jit(solution)/shard_map/while/body/eval_jaxpr/dot_general | solution.py:20
  161.1 0.1 reduce_sum.50
  161.2 0.8 constant_dynamic-slice_fusion.3
  162.0 7.8 %fusion.19 = f32[8,32,512]{2,1,0:T(8,128)S(1)} fusion(bf16[8,32,128,1]{2,1,3,0:T(8,128)(2,1)S(1)} %bitcast.42, bf16[512,32,128]{2,1,0:T(8,128)(2,1)} %bitcast.46), kind=kOutput, calls=%fused_computation.6.clone.1.clone | convolution fusion | flops 1077805056 | bytes 4784128 | tf_op jit(solution)/shard_map/while/body/eval_jaxpr/dot_general | solution.py:20
  169.9 0.1 reduce_sum.50
  170.0 0.2 multiply_reduce_fusion
  170.1 0.1 reduce_sum.43
  170.2 0.6 divide_select_fusion
  170.8 4.4 %all-to-all-start.2 = ((f32[16,4,1]{1,2,0:T(1,128)}), f32[16,4,1]{1,2,0:T(1,128)S(1)}, u32[]{:S(2)}, u32[]{:S(2)}) async-start(f32[16,4,1]{1,2,0:T(1,128)} %bitcast.12), calls=%async_computation.2 | async-start | bytes 16384 | tf_op jit(solution)/shard_map/all_to_all | solution.py:66
  175.2 5.9 %all-to-all-done.2 = f32[16,4,1]{1,2,0:T(1,128)S(1)} async-done(((f32[16,4,1]{1,2,0:T(1,128)}), f32[16,4,1]{1,2,0:T(1,128)S(1)}, u32[]{:S(2)}, u32[]{:S(2)}) %all-to-all-start.2) | async-done | bytes 288 | tf_op jit(solution)/shard_map/all_to_all | solution.py:66
  181.1 0.5 broadcast.75
  181.6 0.7 reduce.5
  182.3 0.1 all_to_all.22
  182.4 0.7 gather_fusion
  183.1 0.0 copy-done
  183.1 0.5 convert_multiply_fusion
  (16 shorter events, 0.1 us)
Async XLA Ops:
  6.5 93.1 %all-gather.2.cloned.1.call-start = ((), (), s32[]{:S(2)}) async-start(), calls=%async_computation.3 | async-start | bytes 4718592 | tf_op jit(solution)/shard_map/all_gather | solution.py:56
  30.3 9.4 %all-to-all-start = ((bf16[16,4,1]{1,2,0:T(2,128)(2,1)}), bf16[16,4,1]{1,2,0:T(2,128)(2,1)S(1)}, u32[]{:S(2)}, u32[]{:S(2)}) async-start(bf16[16,4,1]{1,2,0:T(2,128)(2,1)} %all_to_all.23), calls=%async_computation | async-start | bytes 16384 | tf_op jit(solution)/shard_map/all_to_all | solution.py:52
  99.7 83.4 %copy-start = (s32[32]{0:T(128)S(1)}, s32[32]{0:T(128)}, u32[]{:S(2)}) copy-start(s32[32]{0:T(128)} %param.7) | copy-start | bytes 388
  170.8 10.3 %all-to-all-start.2 = ((f32[16,4,1]{1,2,0:T(1,128)}), f32[16,4,1]{1,2,0:T(1,128)S(1)}, u32[]{:S(2)}, u32[]{:S(2)}) async-start(f32[16,4,1]{1,2,0:T(1,128)} %bitcast.12), calls=%async_computation.2 | async-start | bytes 16384 | tf_op jit(solution)/shard_map/all_to_all | solution.py:66
Sparse Core Ops, SparseCore 0:
  28.2 71.3 all-gather.1
where the time goes:
time: 192 us; the launch traced here: 190 us
  matrix products  62.6 us (33%)
  waiting for transfers between devices  44.1 us (23%)
  blocking collectives  41.5 us (22%)
  local copies, waits for them, and re-layouts  14.3 us (7%)
  between operations  14.1 us (7%)
  starting transfers between devices  7.79 us (4%)
  other arithmetic  5.72 us (3%)
    dot_general x8, matrix products, one_group(): lax.dot_general(queries, flat_visitors, (((1,), (1,)), ((), ())), preferr...  62.6 us
    all_gather x1, waiting for transfers between devices, body(): visitors = lax.all_gather(members, 'blk', axis=0, tiled=True)  34.2 us
    unnamed x1, blocking collectives  25.2 us
    all_to_all x1, blocking collectives, body(): lax.all_to_all(outgoing, 'cluster', split_axis=0, concat_axis=0, tiled=True)  16.4 us
    dynamic_slice x8, local copies, waits for them, and re-layouts, pair_scores(): result = lax.map(one_group, grouped)  6.8 us
    all_to_all x1, waiting for transfers between devices, body(): lax.all_to_all(score, 'cluster', split_axis=0, concat_axis=0, tiled=True)  5.89 us
    all_to_all x1, starting transfers between devices, body(): lax.all_to_all(score, 'cluster', split_axis=0, concat_axis=0, tiled=True)  4.4 us
    all_to_all x1, waiting for transfers between devices, body(): lax.all_to_all(outgoing_flags, 'cluster', split_axis=0, concat_axis=0, ti...  4.01 us
  transfers between devices with their start and end apart: 3, of which 3 were waited for; matrix products, arithmetic and copies ran while one was open for 2% of the time, Pallas kernels for 0%

commit v1 on v0

v1 whole, which is shorter than its diff:
```python
import functools

import jax
import jax.numpy as jnp
from jax import lax
from jax.experimental import pallas as pl
from jax.experimental.pallas import tpu as pltpu
from jax.sharding import PartitionSpec as P

MESH = pl.DeviceIdType.MESH
NT = (((1,), (1,)), ((), ()))
F32 = jnp.float32
TOKS = 32
SOURCES = 16
CAP = 4
ROWS = TOKS * CAP
P_DEV = 32
LANES = 128

OWN, PARTNER, NEXT, PREV = range(4)


def iota(shape, axis):
    return lax.broadcasted_iota(jnp.int32, shape, axis)


def fold_tokens(tile):
    tile = jnp.maximum(tile, pltpu.roll(tile, 4, 1))
    return jnp.maximum(tile, pltpu.roll(tile, 8, 1))


def pair_block(rows_ref, cols_ref, best_ref, row_sums, lane_sums, first, diagonal):
    both = row_sums is not None
    rows = rows_ref[...].reshape(SOURCES * ROWS, LANES)
    width = 2
    steps = 8 // width
    for step in range(steps):
        tiles = []
        for i in range(width):
            cols = cols_ref[:, pl.ds((step * width + i) * 16, 16), :].reshape(256, LANES)
            tiles.append(lax.dot_general(rows, cols, NT, preferred_element_type=F32))
        for tile in tiles:
            best = jnp.max(tile.reshape(SOURCES, 16, 8, 256), axis=1)
            for c in range(SOURCES):
                piece = jnp.maximum(best[c], pltpu.roll(best[c], 4, 0))
                if diagonal:
                    lane = iota((8, 256), 1)
                    same = (lane // 16 == c) & (lane % 4 == iota((8, 256), 0) % 4)
                    piece = jnp.where(same, 0.0, piece)
                lane_sums = lane_sums + piece
        if both:
            top = functools.reduce(jnp.maximum, tiles)
            if step:
                top = jnp.maximum(top, best_ref[...].reshape(SOURCES * ROWS, 256))
            if step < steps - 1:
                best_ref[...] = top.reshape(SOURCES, ROWS, 256)
            else:
                folded = fold_tokens(top[:, :LANES]) + fold_tokens(top[:, LANES:])
                folded = jnp.sum(folded.reshape(SOURCES, 16, 8, LANES), axis=1)
                row_sums[...] = folded if first else row_sums[...] + folded
    return lane_sums


def kernel(emb, lab_ref, keep_ref, out_ref, outgoing, blocks, best, row_sums, results, returned, count, counts,
           plane_count, plane_counts, send_x, recv_x, send_f, recv_f, send_r, recv_r, send_c, recv_c, send_p, recv_p):
    cl, bk = lax.axis_index("cluster"), lax.axis_index("blk")
    y, core = cl // 4, cl % 2
    x, z = (bk // 4) * 2 + (cl // 2) % 2, bk % 4

    def device(x, y, z, core):
        x, y, z, core = x % 4, y % 4, z % 4, core % 2
        return (y * 4 + (x % 2) * 2 + core, (x // 2) * 4 + z)

    def flip(z):
        return jnp.where(z % 4 == 0, 1, 0)

    def ahead(o):
        return device(x + o // 4, y + o % 4, z, core)

    def column(j):
        return device(x, y, z + 4 - j // 2, core + j)

    readers = {
        NEXT: device(x, y, z + 3, core + flip(z + 3)),
        PREV: device(x, y, z + 1, core + 1 + flip(z)),
        PARTNER: device(x, y, z, core + 1),
    }
    homes = {OWN: (z, core), NEXT: (z + 1, core + flip(z)), PREV: (z + 3, core + 1 + flip(z + 3))}

    barrier = pltpu.get_barrier_semaphore()

    def greet(o, _):
        pl.semaphore_signal(barrier, inc=1, device_id=ahead(o), device_id_type=MESH)
        return 0

    def greet_column(j, _):
        pl.semaphore_signal(barrier, inc=1, device_id=column(j), device_id_type=MESH)
        return 0

    lax.fori_loop(1, SOURCES, greet, 0)
    lax.fori_loop(1, 8, greet_column, 0)

    square = (P_DEV, P_DEV)
    on_diagonal = iota(square, 0) == iota(square, 1)

    def to_col(row):
        return jnp.sum(jnp.where(on_diagonal, jnp.broadcast_to(row, square), 0), axis=1, keepdims=True)

    lab_row, keep_row = lab_ref[...], keep_ref[...]
    lab_col, keep_col = to_col(lab_row), to_col(keep_row)
    equal = jnp.broadcast_to(lab_col, square) == jnp.broadcast_to(lab_row, square)
    rank_row = jnp.sum(jnp.where(equal & (iota(square, 0) < iota(square, 1)), 1, 0), axis=0, keepdims=True)
    rank_col = jnp.sum(jnp.where(equal & (iota(square, 1) < iota(square, 0)), 1, 0), axis=1, keepdims=True)

    def offset(label):
        return (((label >> 2) - x) & 3) * 4 + (((label & 3) - y) & 3)

    slot_row = jnp.where(keep_row > 0, offset(lab_row) * CAP + rank_row, -1).astype(F32)

    wide = P_DEV * 16
    spread = (iota((P_DEV, wide), 1) // 16 == iota((P_DEV, wide), 0)).astype(F32)
    slot_lane = jnp.dot(jnp.broadcast_to(slot_row, (8, P_DEV)).astype(jnp.bfloat16), spread.astype(jnp.bfloat16),
                        preferred_element_type=F32)
    code_lane = slot_lane[0:1].astype(jnp.int32) * 16 + iota((1, wide), 1) % 16
    row = iota((64, wide), 0)
    row_code = (row % 4) * 16 + row // 4
    code_lane = jnp.broadcast_to(code_lane, (64, wide))
    hot = jnp.concatenate(
        [(code_lane == row_code + c * 64).astype(F32).astype(jnp.bfloat16) for c in range(SOURCES)], axis=0)
    tokens = jnp.concatenate(
        [emb[:, pl.ds(h * 16, 16), :].reshape(wide, LANES) for h in range(2)], axis=1)
    picked = jnp.dot(hot, tokens, preferred_element_type=F32).astype(jnp.bfloat16)
    for h in range(2):
        half = picked[:, h * LANES:(h + 1) * LANES].reshape(SOURCES, 64, LANES)
        outgoing[:, pl.ds(h * 64, 64), :] = half
        blocks[OWN, 0, pl.ds(h * 64, 64), :] = half[0]
    labelled = jnp.where(iota((P_DEV, LANES), 1) == lab_col, keep_col.astype(F32), 0.0)
    own_count = jnp.sum(labelled, axis=0, keepdims=True)
    count[...] = own_count

    pl.semaphore_wait(barrier, SOURCES - 1 + 7)

    def dispatch(o):
        return pltpu.make_async_remote_copy(outgoing.at[o], blocks.at[OWN, o], send_x.at[o], recv_x.at[o],
                                            device_id=ahead(o), device_id_type=MESH)

    def tell(o):
        return pltpu.make_async_remote_copy(count, counts.at[o], send_c.at[o], recv_c.at[o],
                                            device_id=ahead(o), device_id_type=MESH)

    def tell_column(j):
        return pltpu.make_async_remote_copy(plane_count, plane_counts.at[j], send_p.at[j], recv_p.at[j],
                                            device_id=column(j), device_id_type=MESH)

    def forward(kind, o):
        return pltpu.make_async_remote_copy(blocks.at[OWN, o], blocks.at[kind, o], send_f.at[kind, o],
                                            recv_f.at[kind, o], device_id=readers[kind], device_id_type=MESH)

    def back(k, kind, o):
        plane, c = homes[kind]
        return pltpu.make_async_remote_copy(results.at[k], returned.at[k, o], send_r.at[k, o], recv_r.at[k, o],
                                            device_id=device(x + 4 - o // 4, y + 4 - o % 4, plane, c),
                                            device_id_type=MESH)

    def each(lo, hi, f):
        def step(i, _):
            f(i)
            return 0
        lax.fori_loop(lo, hi, step, 0)

    each(1, SOURCES, lambda o: dispatch(o).start())
    each(1, SOURCES, lambda o: tell(o).start())

    def pass_on(o):
        for kind in (NEXT, PREV, PARTNER):
            forward(kind, o).start()

    pass_on(0)

    def relay(o):
        dispatch(o).wait_recv()
        pass_on(o)

    each(1, SOURCES, relay)

    each(1, SOURCES, lambda o: tell(o).wait_recv())
    total = own_count
    for o in range(1, SOURCES):
        total = total + counts[o]
    plane_count[...] = total
    each(1, 8, lambda j: tell_column(j).start())

    zero = jnp.zeros((8, 256), F32)
    own = blocks.at[OWN]
    lanes_own = pair_block(own, own, best, None, zero, True, True)
    each(0, SOURCES, lambda o: forward(PARTNER, o).wait_recv())
    lanes_own = pair_block(blocks.at[PARTNER], own, best, None, lanes_own, True, False)
    each(0, SOURCES, lambda o: forward(PREV, o).wait_recv())
    lanes_own = pair_block(blocks.at[PREV], own, best, row_sums.at[1], lanes_own, True, False)
    each(0, SOURCES, lambda o: forward(NEXT, o).wait_recv())
    lanes_own = pair_block(blocks.at[NEXT], own, best, row_sums.at[0], lanes_own, True, False)
    lanes_prev = pair_block(blocks.at[NEXT], blocks.at[PREV], best, row_sums.at[0], zero, False, False)

    into = (256, LANES)
    gather = ((iota(into, 0) // 16 == iota(into, 1) // 8) & (iota(into, 0) % 4 == iota(into, 1) % 8)).astype(F32)

    def from_lanes(sums):
        return jnp.dot(sums * 0.5, gather, preferred_element_type=F32, precision=lax.Precision.HIGHEST)

    kept = ((iota((8, LANES), 1) // 4) % 4 == 3).astype(F32)

    def from_rows(sums):
        return lax.dot_general(kept, sums.reshape(SOURCES * 8, LANES), NT, preferred_element_type=F32,
                               precision=lax.Precision.HIGHEST)

    scale = 1.0 / TOKS
    from_own = jnp.sum(from_lanes(lanes_own), axis=0, keepdims=True) * scale
    results[0] = from_own
    results[1] = from_rows(row_sums[0])[0:1] * scale
    results[2] = (from_rows(row_sums[1])[0:1] + jnp.sum(from_lanes(lanes_prev), axis=0, keepdims=True)) * scale
    each(1, SOURCES, lambda o: back(0, OWN, o).start())
    each(0, SOURCES, lambda o: back(1, NEXT, o).start())
    each(0, SOURCES, lambda o: back(2, PREV, o).start())

    each(1, 8, lambda j: tell_column(j).wait_recv())
    for j in range(1, 8):
        total = total + plane_counts[j]

    each(1, SOURCES, lambda o: back(0, OWN, o).wait_recv())
    each(0, SOURCES, lambda o: back(1, NEXT, o).wait_recv())
    each(0, SOURCES, lambda o: back(2, PREV, o).wait_recv())
    lane = iota((1, LANES), 1)
    scores = jnp.zeros((1, LANES), F32)
    for o in range(SOURCES):
        value = (returned[0, o] if o else from_own) + returned[1, o] + returned[2, o]
        scores = jnp.where(lane // 8 == o, value, scores)

    shape = (P_DEV, LANES)
    lane = iota(shape, 1)
    mine = (lane // 8 == offset(lab_col)) & (lane % 4 == rank_col)
    sums = jnp.sum(jnp.where(mine, jnp.broadcast_to(scores, shape), 0.0), axis=1, keepdims=True)
    members = jnp.sum(jnp.where(lane == lab_col, jnp.broadcast_to(total, shape), 0.0), axis=1, keepdims=True)
    keep = keep_col.astype(F32)
    score = keep * (sums / jnp.maximum(members - keep, 1.0))
    out_ref[...] = jnp.sum(jnp.where(on_diagonal, jnp.broadcast_to(score, square), 0.0), axis=0, keepdims=True)

    each(1, SOURCES, lambda o: dispatch(o).wait_send())
    each(1, SOURCES, lambda o: tell(o).wait_send())
    each(1, 8, lambda j: tell_column(j).wait_send())
    for kind in (NEXT, PREV, PARTNER):
        each(0, SOURCES, lambda o: forward(kind, o).wait_send())
    each(1, SOURCES, lambda o: back(0, OWN, o).wait_send())
    each(0, SOURCES, lambda o: back(1, NEXT, o).wait_send())
    each(0, SOURCES, lambda o: back(2, PREV, o).wait_send())


def body(embeds, labels, keep):
    vmem = pl.BlockSpec(memory_space=pltpu.VMEM)
    dma = pltpu.SemaphoreType.DMA
    bf16 = jnp.bfloat16
    out = pl.pallas_call(
        kernel,
        out_shape=jax.ShapeDtypeStruct((1, P_DEV), F32),
        in_specs=[vmem] * 3,
        out_specs=vmem,
        scratch_shapes=[
            pltpu.VMEM((SOURCES, ROWS, LANES), bf16),
            pltpu.VMEM((4, SOURCES, ROWS, LANES), bf16),
            pltpu.VMEM((SOURCES, ROWS, 256), F32),
            pltpu.VMEM((2, SOURCES, 8, LANES), F32),
            pltpu.VMEM((3, 1, LANES), F32),
            pltpu.VMEM((3, SOURCES, 1, LANES), F32),
            pltpu.VMEM((1, LANES), F32),
            pltpu.VMEM((SOURCES, 1, LANES), F32),
            pltpu.VMEM((1, LANES), F32),
            pltpu.VMEM((8, 1, LANES), F32),
            dma((SOURCES,)), dma((SOURCES,)),
            dma((4, SOURCES)), dma((4, SOURCES)),
            dma((3, SOURCES)), dma((3, SOURCES)),
            dma((SOURCES,)), dma((SOURCES,)),
            dma((8,)), dma((8,)),
        ],
        compiler_params=pltpu.CompilerParams(collective_id=0, has_side_effects=True,
                                             vmem_limit_bytes=48 * 1024 * 1024),
        name="pair_scores",
    )(embeds, labels.reshape(1, P_DEV), keep.reshape(1, P_DEV))
    return out.reshape(P_DEV)


def solution(mesh):
    return jax.shard_map(
        body,
        mesh=mesh,
        in_specs=(
            P(("cluster", "blk"), None, None),
            P(("cluster", "blk"), None),
            P(("cluster", "blk")),
        ),
        out_specs=P(("cluster", "blk")),
        check_vma=False,
    )
```

time: 192 us -> 46.9 us (0.24)
  matrix products: 62.6 us -> 0 us
  Pallas kernels: 0 us -> 44.6 us
  waiting for transfers between devices: 44.1 us -> 0 us
  blocking collectives: 41.5 us -> 0 us
  between operations: 14.1 us -> 0.01 us
  local copies, waits for them, and re-layouts: 14.3 us -> 2.13 us
  starting transfers between devices: 7.79 us -> 0 us
  other arithmetic: 5.72 us -> 0 us
    dot_general x8 -> x0, matrix products: 62.6 us -> none  [one_group(): lax.dot_general(queries, flat_visitors, (((1,), (1,)), ((), ())), preferr...]
    pallas_call x0 -> x1, Pallas kernels: none -> 44.6 us  [body(): pl.pallas_call(kernel, out_shape=jax.ShapeDtypeStruct((1, P_DEV), F32), i...]
    all_gather x1 -> x0, waiting for transfers between devices: 34.2 us -> none  [body(): visitors = lax.all_gather(members, 'blk', axis=0, tiled=True)]
    unnamed x1 -> x0, blocking collectives: 25.2 us -> none
    all_to_all x1 -> x0, blocking collectives: 16.4 us -> none  [body(): lax.all_to_all(outgoing, 'cluster', split_axis=0, concat_axis=0, tiled=True)]
    all_to_all x2 -> x0, waiting for transfers between devices: 9.9 us -> none  [the longest x1 5.89 us: body(): lax.all_to_all(score, 'cluster', split_axis=0, concat_axis=0, tiled=True)]
    all_to_all x2 -> x0, starting transfers between devices: 7.79 us -> none  [the longest x1 4.4 us: body(): lax.all_to_all(score, 'cluster', split_axis=0, concat_axis=0, tiled=True)]
    dynamic_slice x8 -> x0, local copies, waits for them, and re-layouts: 6.8 us -> none  [pair_scores(): result = lax.map(one_group, grouped)]
  transfers between devices with their start and end apart: 3 -> 0, of which waited for: 3 -> 0; matrix products, arithmetic and copies ran while one was open for 2% -> 0% of each run, Pallas kernels for 0% -> 0%
where the time goes in v1:
time: 46.9 us; the launch traced here: 46.8 us
  Pallas kernels  44.6 us (95%)
  local copies, waits for them, and re-layouts  2.13 us (5%)
    pallas_call x1, Pallas kernels, body(): pl.pallas_call(kernel, out_shape=jax.ShapeDtypeStruct((1, P_DEV), F32), i...  44.6 us
    unnamed x7, local copies, waits for them, and re-layouts  2.13 us

profile of v1, /device:TPU:0, one launch (start us, length us, event | category | flops | bytes accessed | tf_op | source)
XLA Modules:
  0.0 46.8 jit_solution(3998101360639525251)
XLA Ops:
  0.0 0.0 copy-start.1
  0.0 0.0 copy-start.2
  0.0 0.7 %copy-done.1 = s32[32,1]{0,1:T(1,128)S(1)} copy-done((s32[32,1]{0,1:T(1,128)S(1)}, s32[32,1]{0,1:T(1,128)}, u32[]{:S(2)}) %copy-start.1) | copy-done | bytes 152
  0.7 0.0 copy-done.2
  0.7 0.0 copy-start
  0.7 0.9 %copy-done = bf16[32,32,128]{2,1,0:T(8,128)(2,1)S(1)} copy-done((bf16[32,32,128]{2,1,0:T(8,128)(2,1)S(1)}, bf16[32,32,128]{2,1,0:T(8,128)(2,1)}, u32[]{:S(2)}) %copy-start) | copy-done | bytes 262168
  1.6 44.6 %pair_scores.1 = f32[1,32]{1,0:T(1,128)S(1)} custom-call(bf16[32,32,128]{2,1,0:T(8,128)(2,1)S(1)} %copy-done, s32[1,32]{1,0:T(1,128)S(1)} %bitcast.3, s32[1,32]{1,0:T(1,128)S(1)} %bitcast.4), custom_call_target="tpu_custom_call" | custom-call | tf_op jit(solution)/shard_map/pair_scores/pallas_call | solution.py:261
  46.2 0.5 %copy.5 = f32[32]{0:T(128)} copy(f32[32]{0:T(128)S(1)} %bitcast.5) | data formatting | bytes 256
Async XLA Ops:
  0.0 0.7 %copy-start.1 = (s32[32,1]{0,1:T(1,128)S(1)}, s32[32,1]{0,1:T(1,128)}, u32[]{:S(2)}) copy-start(s32[32,1]{0,1:T(1,128)} %param.4) | copy-start | bytes 388
  0.0 0.7 %copy-start.2 = (s32[32]{0:T(128)S(1)}, s32[32]{0:T(128)}, u32[]{:S(2)}) copy-start(s32[32]{0:T(128)} %param.5) | copy-start | bytes 388
  0.7 0.9 %copy-start = (bf16[32,32,128]{2,1,0:T(8,128)(2,1)S(1)}, bf16[32,32,128]{2,1,0:T(8,128)(2,1)}, u32[]{:S(2)}) copy-start(bf16[32,32,128]{2,1,0:T(8,128)(2,1)} %emb.1) | copy-start | bytes 786436

commit v2 on v1

v2 whole, which is shorter than its diff:
```python
import functools

import jax
import jax.numpy as jnp
from jax import lax
from jax.experimental import pallas as pl
from jax.experimental.pallas import tpu as pltpu
from jax.sharding import PartitionSpec as P

MESH = pl.DeviceIdType.MESH
NT = (((1,), (1,)), ((), ()))
F32 = jnp.float32
TOKS = 32
SOURCES = 16
CAP = 4
ROWS = TOKS * CAP
P_DEV = 32
LANES = 128

OWN, PARTNER, NEXT, PREV = range(4)

ORDER = ((0, 0), (0, 1), (1, 0), (0, 3), (3, 0), (2, 2), (0, 2), (2, 0), (1, 2), (2, 1), (3, 2), (2, 3), (1, 1), (3, 3),
         (1, 3), (3, 1))
HALF = SOURCES // 2
QUARTER = SOURCES // 4


def packed(values, bits):
    word = sum(v << (bits * i) for i, v in enumerate(values))
    return word - (1 << 32) if word >= 1 << 31 else word


X_OF = packed([o[0] for o in ORDER], 2)
Y_OF = packed([o[1] for o in ORDER], 2)
PLACE = [ORDER.index((i // 4, i % 4)) for i in range(SOURCES)]
PLACE_LO, PLACE_HI = packed(PLACE[:8], 4), packed(PLACE[8:], 4)


def x_of(p):
    return (jnp.int32(X_OF) >> (p * 2)) & 3


def y_of(p):
    return (jnp.int32(Y_OF) >> (p * 2)) & 3


def iota(shape, axis):
    return lax.broadcasted_iota(jnp.int32, shape, axis)


def fold_tokens(tile):
    tile = jnp.maximum(tile, pltpu.roll(tile, 4, 1))
    return jnp.maximum(tile, pltpu.roll(tile, 8, 1))


def pair_block(rows_ref, cols_ref, best_ref, row_sums, lane_sums, first, diagonal=None):
    both = row_sums is not None
    n = rows_ref.shape[0]
    rows = rows_ref[...].reshape(n * ROWS, LANES)
    width = 2
    steps = 8 // width
    for step in range(steps):
        tiles = []
        for i in range(width):
            cols = cols_ref[:, pl.ds((step * width + i) * 16, 16), :].reshape(256, LANES)
            tiles.append(lax.dot_general(rows, cols, NT, preferred_element_type=F32))
        for tile in tiles:
            best = jnp.max(tile.reshape(n, 16, 8, 256), axis=1)
            for c in range(n):
                piece = jnp.maximum(best[c], pltpu.roll(best[c], 4, 0))
                if diagonal is not None:
                    lane = iota((8, 256), 1)
                    same = (lane // 16 == c + diagonal) & (lane % 4 == iota((8, 256), 0) % 4)
                    piece = jnp.where(same, 0.0, piece)
                lane_sums = lane_sums + piece
        if both:
            top = functools.reduce(jnp.maximum, tiles)
            if step:
                top = jnp.maximum(top, best_ref[:n].reshape(n * ROWS, 256))
            if step < steps - 1:
                best_ref[:n] = top.reshape(n, ROWS, 256)
            else:
                folded = fold_tokens(top[:, :LANES]) + fold_tokens(top[:, LANES:])
                folded = jnp.sum(folded.reshape(n, 16, 8, LANES), axis=1)
                row_sums[...] = folded if first else row_sums[...] + folded
    return lane_sums


def kernel(emb_in, lab_in, keep_in, out_ref, emb, lab_ref, keep_ref, outgoing, blocks, best, row_sums, results, inbox,
           returned, count, counts, plane_count, plane_counts, load, send_x, recv_x, send_f, recv_f, send_r, recv_r,
           send_o, recv_o, send_c, recv_c, send_p, recv_p):
    cl, bk = lax.axis_index("cluster"), lax.axis_index("blk")
    y, core = cl // 4, cl % 2
    x, z = (bk // 4) * 2 + (cl // 2) % 2, bk % 4

    def device(x, y, z, core):
        x, y, z, core = x % 4, y % 4, z % 4, core % 2
        return (y * 4 + (x % 2) * 2 + core, (x // 2) * 4 + z)

    def flip(z):
        return jnp.where(z % 4 == 0, 1, 0)

    def ahead(o):
        return device(x + x_of(o), y + y_of(o), z, core)

    def column(j):
        return device(x, y, z + 4 - j // 2, core + j)

    readers = {
        NEXT: device(x, y, z + 3, core + flip(z + 3)),
        PREV: device(x, y, z + 1, core + 1 + flip(z)),
        PARTNER: device(x, y, z, core + 1),
    }
    homes = {PARTNER: (z, core + 1), NEXT: (z + 1, core + flip(z)), PREV: (z + 3, core + 1 + flip(z + 3))}

    barrier = pltpu.get_barrier_semaphore()

    def greet(o, _):
        pl.semaphore_signal(barrier, inc=1, device_id=ahead(o), device_id_type=MESH)
        return 0

    def greet_column(j, _):
        pl.semaphore_signal(barrier, inc=1, device_id=column(j), device_id_type=MESH)
        return 0

    lax.fori_loop(1, SOURCES, greet, 0)
    lax.fori_loop(1, 8, greet_column, 0)

    loads = [pltpu.make_async_copy(src, dst, load.at[i])
             for i, (src, dst) in enumerate(((lab_in, lab_ref), (keep_in, keep_ref), (emb_in, emb)))]
    for item in loads:
        item.start()
    loads[0].wait()
    loads[1].wait()

    square = (P_DEV, P_DEV)
    on_diagonal = iota(square, 0) == iota(square, 1)

    def to_col(row):
        return jnp.sum(jnp.where(on_diagonal, jnp.broadcast_to(row, square), 0), axis=1, keepdims=True)

    lab_row, keep_row = lab_ref[...], keep_ref[...]
    lab_col, keep_col = to_col(lab_row), to_col(keep_row)
    equal = jnp.broadcast_to(lab_col, square) == jnp.broadcast_to(lab_row, square)
    rank_row = jnp.sum(jnp.where(equal & (iota(square, 0) < iota(square, 1)), 1, 0), axis=0, keepdims=True)
    rank_col = jnp.sum(jnp.where(equal & (iota(square, 1) < iota(square, 0)), 1, 0), axis=1, keepdims=True)

    def offset(label):
        o = (((label >> 2) - x) & 3) * 4 + (((label & 3) - y) & 3)
        word = jnp.where(o < 8, jnp.int32(PLACE_LO), jnp.int32(PLACE_HI))
        return (word >> ((o & 7) * 4)) & 15

    slot_row = jnp.where(keep_row > 0, offset(lab_row) * CAP + rank_row, -1).astype(F32)

    wide = P_DEV * 16
    spread = (iota((P_DEV, wide), 1) // 16 == iota((P_DEV, wide), 0)).astype(F32)
    slot_lane = jnp.dot(jnp.broadcast_to(slot_row, (8, P_DEV)).astype(jnp.bfloat16), spread.astype(jnp.bfloat16),
                        preferred_element_type=F32)
    code_lane = slot_lane[0:1].astype(jnp.int32) * 16 + iota((1, wide), 1) % 16
    row = iota((64, wide), 0)
    row_code = (row % 4) * 16 + row // 4
    code_lane = jnp.broadcast_to(code_lane, (64, wide))
    hot = jnp.concatenate(
        [(code_lane == row_code + c * 64).astype(F32).astype(jnp.bfloat16) for c in range(SOURCES)], axis=0)
    loads[2].wait()
    tokens = jnp.concatenate(
        [emb[:, pl.ds(h * 16, 16), :].reshape(wide, LANES) for h in range(2)], axis=1)
    picked = jnp.dot(hot, tokens, preferred_element_type=F32).astype(jnp.bfloat16)
    for h in range(2):
        half = picked[:, h * LANES:(h + 1) * LANES].reshape(SOURCES, 64, LANES)
        outgoing[:, pl.ds(h * 64, 64), :] = half
        blocks[OWN, 0, pl.ds(h * 64, 64), :] = half[0]
    labelled = jnp.where(iota((P_DEV, LANES), 1) == lab_col, keep_col.astype(F32), 0.0)
    own_count = jnp.sum(labelled, axis=0, keepdims=True)
    count[...] = own_count

    pl.semaphore_wait(barrier, SOURCES - 1 + 7)

    def dispatch(o):
        return pltpu.make_async_remote_copy(outgoing.at[o], blocks.at[OWN, o], send_x.at[o], recv_x.at[o],
                                            device_id=ahead(o), device_id_type=MESH)

    def tell(o):
        return pltpu.make_async_remote_copy(count, counts.at[o], send_c.at[o], recv_c.at[o],
                                            device_id=ahead(o), device_id_type=MESH)

    def tell_column(j):
        return pltpu.make_async_remote_copy(plane_count, plane_counts.at[j], send_p.at[j], recv_p.at[j],
                                            device_id=column(j), device_id_type=MESH)

    def forward(kind, o):
        return pltpu.make_async_remote_copy(blocks.at[OWN, o], blocks.at[kind, o], send_f.at[kind, o],
                                            recv_f.at[kind, o], device_id=readers[kind], device_id_type=MESH)

    def hand_over(k):
        plane, c = homes[k]
        return pltpu.make_async_remote_copy(results.at[k], inbox.at[k], send_o.at[k], recv_o.at[k],
                                            device_id=device(x, y, plane, c), device_id_type=MESH)

    def back(o):
        return pltpu.make_async_remote_copy(results.at[OWN], returned.at[o], send_r.at[o], recv_r.at[o],
                                            device_id=device(x + 4 - x_of(o), y + 4 - y_of(o), z, core),
                                            device_id_type=MESH)

    def each(lo, hi, f):
        def step(i, _):
            f(i)
            return 0
        lax.fori_loop(lo, hi, step, 0)

    each(1, SOURCES, lambda o: dispatch(o).start())

    def pass_on(o):
        for kind in (PARTNER, NEXT, PREV):
            forward(kind, o).start()

    pass_on(0)

    each(1, SOURCES, lambda o: tell(o).start())

    def relay(o):
        dispatch(o).wait_recv()
        pass_on(o)

    each(1, SOURCES, relay)

    into = (256, LANES)
    gather = ((iota(into, 0) // 16 == iota(into, 1) // 8) & (iota(into, 0) % 4 == iota(into, 1) % 8)).astype(F32)

    def from_lanes(sums):
        return jnp.dot(sums * 0.5, gather, preferred_element_type=F32, precision=lax.Precision.HIGHEST)

    kept = ((iota((8, LANES), 1) // 4) % 4 == 3).astype(F32)

    def from_rows(sums):
        return lax.dot_general(kept, sums.reshape(SOURCES * 8, LANES), NT, preferred_element_type=F32,
                               precision=lax.Precision.HIGHEST)

    scale = 1.0 / TOKS
    zero = jnp.zeros((8, 256), F32)
    own = blocks.at[OWN]

    lanes_own = pair_block(blocks.at[OWN, :HALF], own, best, None, zero, True, 0)

    each(0, SOURCES, lambda o: forward(PARTNER, o).wait_recv())
    part = pl.ds(core * HALF, HALF)
    row_sums[2] = jnp.zeros((SOURCES, 8, LANES), F32)
    lanes_pair = pair_block(blocks.at[core, part], blocks.at[1 - core], best, row_sums.at[2, part], zero, True)
    by_rows = from_rows(row_sums[2])[0:1] * scale
    by_lanes = jnp.sum(from_lanes(lanes_pair), axis=0, keepdims=True) * scale
    from_pair = jnp.where(core == 0, by_rows, by_lanes)
    results[PARTNER] = jnp.where(core == 0, by_lanes, by_rows)
    hand_over(PARTNER).start()

    each(1, SOURCES, lambda o: tell(o).wait_recv())
    total = own_count
    for o in range(1, SOURCES):
        total = total + counts[o]
    plane_count[...] = total
    each(1, 8, lambda j: tell_column(j).start())

    for q in range(0, SOURCES, QUARTER):
        for kind, k in ((PREV, 1), (NEXT, 0)):
            each(q, q + QUARTER, lambda o, kind=kind: forward(kind, o).wait_recv())
            some = pl.ds(q, QUARTER)
            lanes_own = pair_block(blocks.at[kind, some], own, best, row_sums.at[k, some], lanes_own, True)
    lanes_prev = pair_block(blocks.at[NEXT], blocks.at[PREV], best, row_sums.at[0], zero, False)
    results[NEXT] = from_rows(row_sums[0])[0:1] * scale
    results[PREV] = (from_rows(row_sums[1])[0:1] + jnp.sum(from_lanes(lanes_prev), axis=0, keepdims=True)) * scale
    hand_over(NEXT).start()
    hand_over(PREV).start()

    lanes_own = pair_block(blocks.at[OWN, HALF:], own, best, None, lanes_own, True, HALF)
    from_own = jnp.sum(from_lanes(lanes_own), axis=0, keepdims=True) * scale + from_pair
    for kind in (PARTNER, NEXT, PREV):
        hand_over(kind).wait_recv()
        from_own = from_own + inbox[kind]
    results[OWN] = from_own
    each(1, SOURCES, lambda o: back(o).start())

    each(1, 8, lambda j: tell_column(j).wait_recv())
    for j in range(1, 8):
        total = total + plane_counts[j]

    each(1, SOURCES, lambda o: back(o).wait_recv())
    lane = iota((1, LANES), 1)
    scores = jnp.zeros((1, LANES), F32)
    for o in range(SOURCES):
        scores = jnp.where(lane // 8 == o, returned[o] if o else from_own, scores)

    shape = (P_DEV, LANES)
    lane = iota(shape, 1)
    mine = (lane // 8 == offset(lab_col)) & (lane % 4 == rank_col)
    sums = jnp.sum(jnp.where(mine, jnp.broadcast_to(scores, shape), 0.0), axis=1, keepdims=True)
    members = jnp.sum(jnp.where(lane == lab_col, jnp.broadcast_to(total, shape), 0.0), axis=1, keepdims=True)
    keep = keep_col.astype(F32)
    score = keep * (sums / jnp.maximum(members - keep, 1.0))
    out_ref[...] = jnp.sum(jnp.where(on_diagonal, jnp.broadcast_to(score, square), 0.0), axis=0, keepdims=True)

    each(1, SOURCES, lambda o: dispatch(o).wait_send())
    each(1, SOURCES, lambda o: tell(o).wait_send())
    each(1, 8, lambda j: tell_column(j).wait_send())
    for kind in (PARTNER, NEXT, PREV):
        each(0, SOURCES, lambda o: forward(kind, o).wait_send())
    for kind in (PARTNER, NEXT, PREV):
        hand_over(kind).wait_send()
    each(1, SOURCES, lambda o: back(o).wait_send())


def body(embeds, labels, keep):
    vmem = pl.BlockSpec(memory_space=pltpu.VMEM)
    dma = pltpu.SemaphoreType.DMA
    bf16 = jnp.bfloat16
    out = pl.pallas_call(
        kernel,
        out_shape=jax.ShapeDtypeStruct((1, P_DEV), F32),
        in_specs=[pl.BlockSpec(memory_space=pltpu.HBM)] * 3,
        out_specs=vmem,
        scratch_shapes=[
            pltpu.VMEM((P_DEV, TOKS, LANES), bf16),
            pltpu.VMEM((1, P_DEV), jnp.int32),
            pltpu.VMEM((1, P_DEV), jnp.int32),
            pltpu.VMEM((SOURCES, ROWS, LANES), bf16),
            pltpu.VMEM((4, SOURCES, ROWS, LANES), bf16),
            pltpu.VMEM((SOURCES, ROWS, 256), F32),
            pltpu.VMEM((3, SOURCES, 8, LANES), F32),
            pltpu.VMEM((4, 1, LANES), F32),
            pltpu.VMEM((4, 1, LANES), F32),
            pltpu.VMEM((SOURCES, 1, LANES), F32),
            pltpu.VMEM((1, LANES), F32),
            pltpu.VMEM((SOURCES, 1, LANES), F32),
            pltpu.VMEM((1, LANES), F32),
            pltpu.VMEM((8, 1, LANES), F32),
            dma((3,)),
            dma((SOURCES,)), dma((SOURCES,)),
            dma((4, SOURCES)), dma((4, SOURCES)),
            dma((SOURCES,)), dma((SOURCES,)),
            dma((4,)), dma((4,)),
            dma((SOURCES,)), dma((SOURCES,)),
            dma((8,)), dma((8,)),
        ],
        compiler_params=pltpu.CompilerParams(collective_id=0, has_side_effects=True,
                                             vmem_limit_bytes=48 * 1024 * 1024),
        name="pair_scores",
    )(embeds, labels.reshape(1, P_DEV), keep.reshape(1, P_DEV))
    return out.reshape(P_DEV)


def solution(mesh):
    return jax.shard_map(
        body,
        mesh=mesh,
        in_specs=(
            P(("cluster", "blk"), None, None),
            P(("cluster", "blk"), None),
            P(("cluster", "blk")),
        ),
        out_specs=P(("cluster", "blk")),
        check_vma=False,
    )
```

time: 46.9 us -> 43.8 us (0.934)
  Pallas kernels: 44.6 us -> 41.5 us
    pallas_call x1, Pallas kernels: 44.6 us -> 41.5 us  [body(): pl.pallas_call(kernel, out_shape=jax.ShapeDtypeStruct((1, P_DEV), F32), i...]
where the time goes in v2:
time: 43.8 us; the launch traced here: 43.6 us
  Pallas kernels  41.5 us (95%)
  local copies, waits for them, and re-layouts  2.13 us (5%)
    pallas_call x1, Pallas kernels, body(): pl.pallas_call(kernel, out_shape=jax.ShapeDtypeStruct((1, P_DEV), F32), i...  41.5 us
    unnamed x7, local copies, waits for them, and re-layouts  2.13 us

profile of v2, /device:TPU:0, one launch (start us, length us, event | category | flops | bytes accessed | tf_op | source)
XLA Modules:
  0.0 43.6 jit_solution(17430787683409565132)
XLA Ops:
  0.0 0.0 copy-start.1
  0.0 0.0 copy-start.2
  0.0 0.7 %copy-done.1 = s32[32,1]{0,1:T(1,128)S(1)} copy-done((s32[32,1]{0,1:T(1,128)S(1)}, s32[32,1]{0,1:T(1,128)}, u32[]{:S(2)}) %copy-start.1) | copy-done | bytes 152
  0.7 0.0 copy-done.2
  0.7 0.0 copy-start
  0.7 0.9 %copy-done = bf16[32,32,128]{2,1,0:T(8,128)(2,1)S(1)} copy-done((bf16[32,32,128]{2,1,0:T(8,128)(2,1)S(1)}, bf16[32,32,128]{2,1,0:T(8,128)(2,1)}, u32[]{:S(2)}) %copy-start) | copy-done | bytes 262168
  1.6 41.5 %pair_scores.1 = f32[1,32]{1,0:T(1,128)S(1)} custom-call(bf16[32,32,128]{2,1,0:T(8,128)(2,1)S(1)} %copy-done, s32[1,32]{1,0:T(1,128)S(1)} %bitcast.3, s32[1,32]{1,0:T(1,128)S(1)} %bitcast.4), custom_call_target="tpu_custom_call" | custom-call | tf_op jit(solution)/shard_map/pair_scores/pallas_call | solution.py:314
  43.1 0.5 %copy.5 = f32[32]{0:T(128)} copy(f32[32]{0:T(128)S(1)} %bitcast.5) | data formatting | bytes 256
Async XLA Ops:
  0.0 0.7 %copy-start.1 = (s32[32,1]{0,1:T(1,128)S(1)}, s32[32,1]{0,1:T(1,128)}, u32[]{:S(2)}) copy-start(s32[32,1]{0,1:T(1,128)} %param.4) | copy-start | bytes 388
  0.0 0.7 %copy-start.2 = (s32[32]{0:T(128)S(1)}, s32[32]{0:T(128)}, u32[]{:S(2)}) copy-start(s32[32]{0:T(128)} %param.5) | copy-start | bytes 388
  0.7 0.9 %copy-start = (bf16[32,32,128]{2,1,0:T(8,128)(2,1)S(1)}, bf16[32,32,128]{2,1,0:T(8,128)(2,1)}, u32[]{:S(2)}) copy-start(bf16[32,32,128]{2,1,0:T(8,128)(2,1)} %emb_in.1) | copy-start | bytes 786436

commit v3 on v2

--- a/solution.py
+++ b/solution.py
@@ -22,7 +22,7 @@
 ORDER = ((0, 0), (0, 1), (1, 0), (0, 3), (3, 0), (2, 2), (0, 2), (2, 0), (1, 2), (2, 1), (3, 2), (2, 3), (1, 1), (3, 3),
          (1, 3), (3, 1))
 HALF = SOURCES // 2
-QUARTER = SOURCES // 4
+QUARTER = SOURCES // 2
 
 
 def packed(values, bits):
@@ -211,7 +211,7 @@
     each(1, SOURCES, lambda o: dispatch(o).start())
 
     def pass_on(o):
-        for kind in (PARTNER, NEXT, PREV):
+        for kind in (NEXT, PREV, PARTNER):
             forward(kind, o).start()
 
     pass_on(0)

time: 43.8 us -> 42.8 us (0.977)
  Pallas kernels: 41.5 us -> 40.5 us
    pallas_call x1, Pallas kernels: 41.5 us -> 40.5 us  [body(): pl.pallas_call(kernel, out_shape=jax.ShapeDtypeStruct((1, P_DEV), F32), i...]
where the time goes in v3:
time: 42.8 us; the launch traced here: 42.6 us
  Pallas kernels  40.5 us (95%)
  local copies, waits for them, and re-layouts  2.13 us (5%)
    pallas_call x1, Pallas kernels, body(): pl.pallas_call(kernel, out_shape=jax.ShapeDtypeStruct((1, P_DEV), F32), i...  40.5 us
    unnamed x7, local copies, waits for them, and re-layouts  2.13 us

profile of v3, /device:TPU:0, one launch (start us, length us, event | category | flops | bytes accessed | tf_op | source)
XLA Modules:
  0.0 42.6 jit_solution(14126405034877667125)
XLA Ops:
  0.0 0.0 copy-start.1
  0.0 0.0 copy-start.2
  0.0 0.7 %copy-done.1 = s32[32,1]{0,1:T(1,128)S(1)} copy-done((s32[32,1]{0,1:T(1,128)S(1)}, s32[32,1]{0,1:T(1,128)}, u32[]{:S(2)}) %copy-start.1) | copy-done | bytes 152
  0.7 0.0 copy-done.2
  0.7 0.0 copy-start
  0.7 0.9 %copy-done = bf16[32,32,128]{2,1,0:T(8,128)(2,1)S(1)} copy-done((bf16[32,32,128]{2,1,0:T(8,128)(2,1)S(1)}, bf16[32,32,128]{2,1,0:T(8,128)(2,1)}, u32[]{:S(2)}) %copy-start) | copy-done | bytes 262168
  1.6 40.5 %pair_scores.1 = f32[1,32]{1,0:T(1,128)S(1)} custom-call(bf16[32,32,128]{2,1,0:T(8,128)(2,1)S(1)} %copy-done, s32[1,32]{1,0:T(1,128)S(1)} %bitcast.3, s32[1,32]{1,0:T(1,128)S(1)} %bitcast.4), custom_call_target="tpu_custom_call" | custom-call | tf_op jit(solution)/shard_map/pair_scores/pallas_call | solution.py:314
  42.1 0.5 %copy.5 = f32[32]{0:T(128)} copy(f32[32]{0:T(128)S(1)} %bitcast.5) | data formatting | bytes 256
Async XLA Ops:
  0.0 0.7 %copy-start.1 = (s32[32,1]{0,1:T(1,128)S(1)}, s32[32,1]{0,1:T(1,128)}, u32[]{:S(2)}) copy-start(s32[32,1]{0,1:T(1,128)} %param.4) | copy-start | bytes 388
  0.0 0.7 %copy-start.2 = (s32[32]{0:T(128)S(1)}, s32[32]{0:T(128)}, u32[]{:S(2)}) copy-start(s32[32]{0:T(128)} %param.5) | copy-start | bytes 388
  0.7 0.9 %copy-start = (bf16[32,32,128]{2,1,0:T(8,128)(2,1)S(1)}, bf16[32,32,128]{2,1,0:T(8,128)(2,1)}, u32[]{:S(2)}) copy-start(bf16[32,32,128]{2,1,0:T(8,128)(2,1)} %emb_in.1) | copy-start | bytes 786436
